TPU v7x, 256 devices: a whole 4x4x8 slice. The times are simulated.
256 devices in a mesh: member: 2 (over y_lo), lat: 4 (over x), lon: 32 (over z, y_hi, core).
Axes of the slice: x: 4, y: 4 (y_hi: 2, y_lo: 2; y = y_hi * 2 + y_lo), z: 8, core: 2. Of those that a mesh axis runs over, the one named last changes fastest.
Arguments:
- features: bfloat16 [2, 720, 1440, 128], P('member', 'lat', 'lon'), may hold values from -6 to 6
- present_condition: bfloat16 [2, 720, 1440, 80], P('member', 'lat', 'lon'), may hold values from -6 to 6
- target: bfloat16 [720, 1440, 80], P('lat', 'lon'), may hold values from -8 to 8
- filter_weights_tensor: bfloat16 [3, 3, 128, 80], replicated, may hold values from -0.1875 to 0.1875
Outputs:
- predicted_outputs: bfloat16 [2, 720, 1440, 80], P('member', 'lat', 'lon')
- objective_mean: float32 [], replicated
- hidden_state_slope: bfloat16 [2, 720, 1440, 128], P('member', 'lat', 'lon')
- filter_weights_slope: float32 [3, 3, 128, 80], replicated
All inputs are finite; a program needn't handle non-finite values.
Results may differ from a plain program's by a relative error of at most 0.0095.
Values may be sent and summed in bfloat16 or wider, within the bound.
No kernel may reach another device: no remote copies, remote signals or barrier semaphores. Data moves between devices by JAX's collectives and lax.ppermute only.
A program may use at most 128 MiB of HBM per device.

v0:
```python
import math
import jax
import jax.numpy as jnp
from jax import lax
from jax.sharding import PartitionSpec as P

epsilon = 1e-06


def padded(block, sides, width, periodic):
    for axis, dim in sides:
        count = lax.axis_size(axis)
        forward = [(i, i + 1) for i in range(count - 1)]
        if periodic:
            forward.append((count - 1, 0))
        backward = [(target, source) for source, target in forward]
        low = lax.ppermute(
            lax.slice_in_dim(block, block.shape[dim] - width, None, axis=dim), axis, forward
        )
        high = lax.ppermute(lax.slice_in_dim(block, 0, width, axis=dim), axis, backward)
        block = jnp.concatenate([low, block, high], axis=dim)
    return block


def partner(value, axis, distance):
    mask = 2**distance
    pairs = [(source, source ^ mask) for source in range(lax.axis_size(axis))]
    return lax.ppermute(value, axis, pairs)


def stencil_filter_step(haloed_grid_array, weights_hwio):
    result = lax.conv_general_dilated(
        haloed_grid_array[None],
        weights_hwio,
        (1, 1),
        "VALID",
        dimension_numbers=("NHWC", "HWIO", "NHWC"),
        preferred_element_type=jnp.float32,
    )
    return result[0]


def latitude_weights(row_index, total_rows):
    scale = math.pi / total_rows
    angles = 0.5 * math.pi - (row_index.astype(jnp.float32) + 0.5) * scale
    every_row = (
        0.5 * math.pi - (jnp.arange(total_rows, dtype=jnp.int32).astype(jnp.float32) + 0.5) * scale
    )
    return jnp.cos(angles) / jnp.mean(jnp.cos(every_row))


def tap_products(haloed_grid_array, cotangent):
    lat_rows, lon_cols, channels = cotangent.shape
    inputs = haloed_grid_array.shape[2]
    flat_grad = cotangent.reshape(lat_rows * lon_cols, channels)
    stacked = []
    for row_tap in range(3):
        across = []
        for col_tap in range(3):
            window = haloed_grid_array[
                row_tap : row_tap + lat_rows, col_tap : col_tap + lon_cols
            ].reshape(lat_rows * lon_cols, inputs)
            across.append(
                lax.dot_general(
                    window, flat_grad, (((0,), (0,)), ((), ())), preferred_element_type=jnp.float32
                )
            )
        stacked.append(jnp.stack(across))
    return jnp.stack(stacked)


def extend_features(field):
    widened = padded(field, (("lon", 1),), 1, True)
    return padded(widened, (("lat", 0),), 1, False)


def extend_cotangent(field):
    widened = padded(field, (("lon", 1),), 1, True)
    return padded(widened, (("lat", 0),), 1, False)


def local(features, present_condition, target, filter_weights_tensor):
    lat_rows = features.shape[1]
    lon_cols = features.shape[2]
    total_rows = lat_rows * lax.axis_size("lat")
    total_cols = lon_cols * lax.axis_size("lon")
    haloed_grid_array = extend_features(features[0])
    predicted_outputs = (
        present_condition[0].astype(jnp.float32)
        + stencil_filter_step(haloed_grid_array, filter_weights_tensor)
    ).astype(jnp.bfloat16)
    companion_sample = partner(predicted_outputs, "member", 0)
    truth = target.astype(jnp.float32)
    energy_metrics = predicted_outputs.astype(jnp.float32)
    misfit = energy_metrics - truth
    errors = jnp.sqrt(jnp.sum(misfit * misfit, axis=-1) + epsilon)
    spread = energy_metrics - companion_sample.astype(jnp.float32)
    pair = jnp.sqrt(jnp.sum(spread * spread, axis=-1) + epsilon)
    row_index = lax.axis_index("lat") * lat_rows + jnp.arange(lat_rows, dtype=jnp.int32)
    weights = latitude_weights(row_index, total_rows)[:, None]
    local_total = jnp.sum(weights * (0.5 * errors - 0.25 * pair))
    cotangent = (
        weights[..., None] * (0.5 * misfit / errors[..., None] - 0.5 * spread / pair[..., None])
    ).astype(jnp.bfloat16)
    flipped = jnp.transpose(filter_weights_tensor[::-1, ::-1], (0, 1, 3, 2))
    hidden_state_slope = stencil_filter_step(extend_cotangent(cotangent), flipped).astype(
        jnp.bfloat16
    )
    partial_grad = tap_products(haloed_grid_array, cotangent)
    summed_grad, total = lax.psum((partial_grad, local_total), ("member", "lat", "lon"))
    objective_mean = total / (total_rows * total_cols)
    filter_weights_slope = summed_grad / math.sqrt(2.0 * total_rows * total_cols)
    return (predicted_outputs[None], objective_mean, hidden_state_slope[None], filter_weights_slope)


def solution(mesh):
    in_specs = (
        P("member", "lat", "lon", None),
        P("member", "lat", "lon", None),
        P("lat", "lon", None),
        P(),
    )
    out_specs = (P("member", "lat", "lon", None), P(), P("member", "lat", "lon", None), P())
    return jax.shard_map(local, mesh=mesh, in_specs=in_specs, out_specs=out_specs, check_vma=False)
```

profile of v0, /device:TPU:1, one launch (start us, length us, event | category | flops | bytes accessed | tf_op | source)
XLA Modules:
  0.0 395.3 jit_solution(8616252345672613163)
XLA Ops:
  7.2 0.0 copy-start
  7.2 0.0 all-reduce.2.cloned.1.call-start
  7.2 1.0 fusion.76
  8.2 4.4 %collective-permute-start = (bf16[180,1,128]{2,0,1:T(8,128)(2,1)S(1)}, bf16[180,1,128]{2,0,1:T(8,128)(2,1)S(1)}, u32[]{:S(2)}, u32[]{:S(2)}) collective-permute-start(bf16[180,1,128]{2,0,1:T(8,128)(2,1)S(1)} %get-tuple-element.10), channel_id=1, source_target_pairs={{0,1},{1,2},{2,3},{3,4},{4,5},{5,6},{6,7},{7,8},{8,9},{9,10},{10,1... | collective-permute-start | bytes 138248 | tf_op jit(solution)/shard_map/ppermute | solution.py:17
  12.6 1.2 collective-permute-done
  13.7 3.8 collective-permute-done.1
  17.6 1.0 pad_maximum_fusion.5
  18.6 3.1 collective-permute-start.2
  21.7 1.3 collective-permute-start.3
  23.0 3.3 collective-permute-done.3
  26.3 1.0 maximum_bitcast_fusion
  27.3 0.2 pad
  27.5 0.0 copy-start.10
  27.5 0.6 copy.17
  28.1 0.2 slice.78
  28.3 6.8 %broadcast_select_fusion = f32[180,8,6,80]{3,1,2,0:T(8,128)} fusion(pred[8,6]{0,1:T(8,128)(4,1)S(1)} %copy-done.10, bf16[3,3,128,80]{2,3,1,0:T(8,128)(2,1)S(1)} %copy-done, bf16[182,1,7,2,128]{4,2,3,0,1:T(8,128)(2,1)S(1)} %slice.78, bf16[182,1,8,6,128]{4,2,3,0,1:T(8,128)(2,1)S(1)} %copy.17), kind=kOutput, calls=%fused_computation.28 | convolution fusion | flops 1602161664 | bytes 5837872 | tf_op jit(solution)/shard_map/conv_general_dilated | solution.py:32
  35.1 6.2 %copy.18 = f32[180,8,6,80]{0,3,2,1:T(8,128)} copy(f32[180,8,6,80]{3,1,2,0:T(8,128)} %broadcast_select_fusion) | data formatting | bytes 5529600 | tf_op jit(solution)/shard_map/conv_general_dilated | solution.py:32
  41.3 4.4 %fusion.3 = bf16[1,180,45,80]{1,3,2,0:T(8,128)(2,1)} fusion(f32[180,1,48,80]{0,3,2,1:T(8,128)} %bitcast.83, bf16[1,180,45,80]{1,3,2,0:T(8,128)(2,1)} %param.5), kind=kLoop, calls=%fused_computation.9 | loop fusion | flops 1944000 | bytes 5184000 | tf_op jit(solution)/shard_map/convert_element_type | solution.py:91
  45.7 0.4 collective-permute-start.4
  46.1 1.7 copy.27
  47.8 4.2 %reshape_squeeze.3 = bf16[8100,128]{1,0:T(8,128)(2,1)} reshape(bf16[1,180,45,128]{3,2,1,0:T(8,128)(2,1)} %copy.27) | data formatting | bytes 4147200 | tf_op jit(solution)/shard_map/reshape;squeeze | solution.py:62
  52.0 0.6 cosine_reduce_fusion
  53.3 0.1 cosine_divide_fusion
  53.4 4.4 %maximum_maximum_fusion = (bf16[181,47,128]{2,0,1:T(8,128)(2,1)}, bf16[181,47,128]{2,0,1:T(8,128)(2,1)}) fusion(bf16[180,1,128]{2,0,1:T(8,128)(2,1)S(1)} %collective-permute-done.1, bf16[180,45,128]{2,0,1:T(8,128)(2,1)S(1)} %bitcast.80, bf16[180,1,128]{2,0,1:T(8,128)(2,1)S(1)} %collective-permute-done, bf16[1,47,128]{2,0,1:T(2,128)(2,1)S(1)} %collective-permute-done.2, ...), kind=kLoop, calls=%fused_computation.26 | loop fusion | flops 17422336 | bytes 6545408 | tf_op jit(solution)/shard_map/concatenate | solution.py:21
  57.8 26.6 %collective-permute-done.4 = bf16[180,45,80]{0,2,1:T(8,128)(2,1)} collective-permute-done((bf16[180,45,80]{0,2,1:T(8,128)(2,1)}, bf16[180,45,80]{0,2,1:T(8,128)(2,1)}, u32[]{:S(2)}, u32[]{:S(2)}) %collective-permute-start.4) | collective-permute-done | bytes 1296032 | tf_op jit(solution)/shard_map/ppermute | solution.py:28
  84.3 3.6 multiply_reduce_fusion
  87.9 0.6 add_sqrt_fusion.1
  88.6 4.8 %multiply_convert_fusion = bf16[180,45,80]{0,2,1:T(8,128)(2,1)} fusion(bf16[180,45,80]{0,2,1:T(8,128)(2,1)S(1)} %copy-done.5, bf16[180,45,80]{0,2,1:T(8,128)(2,1)} %collective-permute-done.4, f32[180,45]{0,1:T(8,128)S(1)} %get-tuple-element.18, f32[180,45]{0,1:T(8,128)S(1)} %get-tuple-element.16, f32[180]{0:T(256)S(1)} %cosine_divide_fusion, ...), kind=kLoop, calls=%fused_computation.10 | loop fusion | flops 7776000 | bytes 5249520 | tf_op jit(solution)/shard_map/convert_element_type | solution.py:104
  93.4 4.7 %copy.26 = bf16[180,45,80]{2,1,0:T(8,128)(2,1)} copy(bf16[180,45,80]{0,2,1:T(8,128)(2,1)} %multiply_convert_fusion) | data formatting | bytes 2592000 | tf_op jit(solution)/shard_map/convert_element_type | solution.py:104
  98.1 3.0 fusion.44
  101.1 0.3 copy-done.7
  101.5 0.8 fusion.47
  102.2 0.8 fusion.50
  103.0 0.8 copy-done.6
  103.9 1.3 fusion.53
  105.1 1.3 fusion.56
  106.4 1.3 fusion.59
  107.7 4.3 %reshape.50 = bf16[8100,80]{1,0:T(8,128)(2,1)} reshape(bf16[180,45,80]{2,1,0:T(8,128)(2,1)} %copy.26) | data formatting | bytes 2592000 | tf_op jit(solution)/shard_map/reshape | solution.py:55
  112.0 5.5 %collective-permute-start.5 = (bf16[180,1,80]{0,2,1:T(8,128)(2,1)S(1)}, bf16[180,1,80]{0,2,1:T(8,128)(2,1)S(1)}, u32[]{:S(2)}, u32[]{:S(2)}) collective-permute-start(bf16[180,1,80]{0,2,1:T(8,128)(2,1)S(1)} %get-tuple-element.14), channel_id=1, source_target_pairs={{0,1},{1,2},{2,3},{3,4},{4,5},{5,6},{6,7},{7,8},{8,9},{9,10},{10,1... | collective-permute-start | bytes 86408 | tf_op jit(solution)/shard_map/ppermute | solution.py:17
  117.5 2.9 convolution_bitcast_fusion
  120.4 0.8 fusion.62
  121.2 0.8 fusion.65
  122.1 0.3 collective-permute-done.6
  122.4 0.6 copy-done.8
  123.0 0.4 pad_maximum_fusion.1
  123.4 1.4 fusion.77
  124.8 1.6 copy.19
  126.4 3.2 collective-permute-start.7
  129.6 0.4 copy.20
  130.1 1.3 collective-permute-start.8
  131.4 0.8 pad_maximum_fusion.2
  132.1 0.0 all-reduce.2.cloned.1.call-update
  132.2 81.6 %psum.14 = f32[]{:T(128)} all-reduce(f32[]{:T(128)} %get-tuple-element.17), channel_id=1, replica_groups=mesh['member'=2,'lat'=4,'lon'=32] {'member','lat','lon'}, use_global_device_ids=true, to_apply=%region_4.0 | all-reduce | flops 1 | bytes 8 | tf_op jit(solution)/shard_map/psum | solution.py:110
  214.5 0.5 copy.21
  215.0 1.4 copy.22
  216.3 2.4 maximum_bitcast_fusion.1
  218.8 0.4 pad.2
  219.1 3.4 copy.24
  222.5 1.3 slice.84
  223.8 7.1 %select_convert_fusion = bf16[180,8,6,128]{3,1,2,0:T(8,128)(2,1)S(1)} fusion(pred[8,6]{0,1:T(8,128)(4,1)S(1)} %copy-done.11, bf16[3,3,128,80]{2,3,1,0:T(8,128)(2,1)S(1)} %copy-done, bf16[182,1,7,2,80]{4,2,3,0,1:T(8,128)(2,1)S(1)} %slice.84, bf16[182,1,8,6,80]{4,2,3,0,1:T(8,128)(2,1)} %copy.24), kind=kOutput, calls=%fused_computation.6 | convolution fusion | flops 1600327680 | bytes 4201648 | tf_op jit(solution)/shard_map/conv_general_dilated | solution.py:32
  231.0 0.6 copy.25
  231.6 1.5 slice_bitcast_fusion.1
  233.1 152.1 %all-reduce.2.cloned.1.call-done = f32[3,3,128,80]{2,3,1,0:T(8,128)} async-done(((f32[3,3,128,80]{2,3,1,0:T(8,128)}), f32[3,3,128,80]{2,3,1,0:T(8,128)}) %all-reduce.2.cloned.1.call-update) | async-done | bytes 368656 | tf_op jit(solution)/shard_map/psum | solution.py:110
  385.2 1.8 broadcast_multiply_fusion
  (28 shorter events, 0.1 us)
Async XLA Ops:
  7.2 21.1 %copy-start = (bf16[3,3,128,80]{2,3,1,0:T(8,128)(2,1)S(1)}, bf16[3,3,128,80]{2,3,1,0:T(8,128)(2,1)}, u32[]{:S(2)}) copy-start(bf16[3,3,128,80]{2,3,1,0:T(8,128)(2,1)} %param.7) | copy-start | bytes 552964
  7.2 19.1 %copy-start.1 = (bf16[1,180,45,128]{3,1,2,0:T(8,128)(2,1)S(1)}, bf16[1,180,45,128]{3,1,2,0:T(8,128)(2,1)}, u32[]{:S(2)}) copy-start(bf16[1,180,45,128]{3,1,2,0:T(8,128)(2,1)} %param.4) | copy-start | bytes 6220804
  7.2 378.0 %all-reduce.2.cloned.1.call-start = ((), (), s32[]{:S(2)}) async-start(), calls=%async_computation | async-start | bytes 737280 | tf_op jit(solution)/shard_map/psum | solution.py:110
  8.2 5.5 %collective-permute-start = (bf16[180,1,128]{2,0,1:T(8,128)(2,1)S(1)}, bf16[180,1,128]{2,0,1:T(8,128)(2,1)S(1)}, u32[]{:S(2)}, u32[]{:S(2)}) collective-permute-start(bf16[180,1,128]{2,0,1:T(8,128)(2,1)S(1)} %get-tuple-element.10), channel_id=1, source_target_pairs={{0,1},{1,2},{2,3},{3,4},{4,5},{5,6},{6,7},{7,8},{8,9},{9,10},{10,1... | collective-permute-start | bytes 138248 | tf_op jit(solution)/shard_map/ppermute | solution.py:17
  12.6 5.0 %collective-permute-start.1 = (bf16[180,1,128]{2,0,1:T(8,128)(2,1)S(1)}, bf16[180,1,128]{2,0,1:T(8,128)(2,1)S(1)}, u32[]{:S(2)}, u32[]{:S(2)}) collective-permute-start(bf16[180,1,128]{2,0,1:T(8,128)(2,1)S(1)} %get-tuple-element.11), channel_id=1, source_target_pairs={{1,0},{2,1},{3,2},{4,3},{5,4},{6,5},{7,6},{8,7},{9,8},{10,9},{11,1... | collective-permute-start | bytes 138248 | tf_op jit(solution)/shard_map/ppermute | solution.py:20
  18.6 4.4 %collective-permute-start.2 = (bf16[1,47,128]{2,0,1:T(2,128)(2,1)S(1)}, bf16[1,47,128]{2,0,1:T(2,128)(2,1)S(1)}, u32[]{:S(2)}, u32[]{:S(2)}) collective-permute-start(bf16[1,47,128]{2,0,1:T(2,128)(2,1)S(1)} %get-tuple-element.8), channel_id=1, source_target_pairs={{0,32},{32,64},{64,96},{1,33},{33,65},{65,97},{2,34},{34,66},{66,9... | collective-permute-start | bytes 36104 | tf_op jit(solution)/shard_map/ppermute | solution.py:17
  21.7 4.6 %collective-permute-start.3 = (bf16[1,47,128]{2,0,1:T(2,128)(2,1)S(1)}, bf16[1,47,128]{2,0,1:T(2,128)(2,1)S(1)}, u32[]{:S(2)}, u32[]{:S(2)}) collective-permute-start(bf16[1,47,128]{2,0,1:T(2,128)(2,1)S(1)} %get-tuple-element.9), channel_id=1, source_target_pairs={{32,0},{64,32},{96,64},{33,1},{65,33},{97,65},{34,2},{66,34},{98,6... | collective-permute-start | bytes 36104 | tf_op jit(solution)/shard_map/ppermute | solution.py:20
  27.5 0.8 copy-start.10
  45.7 38.6 %collective-permute-start.4 = (bf16[180,45,80]{0,2,1:T(8,128)(2,1)}, bf16[180,45,80]{0,2,1:T(8,128)(2,1)}, u32[]{:S(2)}, u32[]{:S(2)}) collective-permute-start(bf16[180,45,80]{0,2,1:T(8,128)(2,1)} %bitcast.6), channel_id=1, source_target_pairs={{0,128},{128,0},{1,129},{129,1},{2,130},{130,2},{3,131},{131,3},{4... | collective-permute-start | bytes 3888008 | tf_op jit(solution)/shard_map/ppermute | solution.py:28
  53.4 31.0 %copy-start.5 = (bf16[180,45,80]{0,2,1:T(8,128)(2,1)S(1)}, bf16[180,45,80]{0,2,1:T(8,128)(2,1)}, u32[]{:S(2)}) copy-start(bf16[180,45,80]{0,2,1:T(8,128)(2,1)} %param.6) | copy-start | bytes 3888004
  98.1 3.0 copy-start.2
  98.1 3.4 copy-start.7
  102.2 1.6 copy-start.6
  112.0 8.4 %copy-start.3 = (bf16[180,45,80]{0,2,1:T(8,128)(2,1)S(1)}, bf16[180,45,80]{0,2,1:T(8,128)(2,1)}, u32[]{:S(2)}) copy-start(bf16[180,45,80]{0,2,1:T(8,128)(2,1)} %multiply_convert_fusion) | copy-start | bytes 3888004
  112.0 10.1 %collective-permute-start.5 = (bf16[180,1,80]{0,2,1:T(8,128)(2,1)S(1)}, bf16[180,1,80]{0,2,1:T(8,128)(2,1)S(1)}, u32[]{:S(2)}, u32[]{:S(2)}) collective-permute-start(bf16[180,1,80]{0,2,1:T(8,128)(2,1)S(1)} %get-tuple-element.14), channel_id=1, source_target_pairs={{0,1},{1,2},{2,3},{3,4},{4,5},{5,6},{6,7},{7,8},{8,9},{9,10},{10,1... | collective-permute-start | bytes 86408 | tf_op jit(solution)/shard_map/ppermute | solution.py:17
  117.5 4.9 %collective-permute-start.6 = (bf16[180,1,80]{0,2,1:T(8,128)(2,1)S(1)}, bf16[180,1,80]{0,2,1:T(8,128)(2,1)S(1)}, u32[]{:S(2)}, u32[]{:S(2)}) collective-permute-start(bf16[180,1,80]{0,2,1:T(8,128)(2,1)S(1)} %get-tuple-element.15), channel_id=1, source_target_pairs={{1,0},{2,1},{3,2},{4,3},{5,4},{6,5},{7,6},{8,7},{9,8},{10,9},{11,1... | collective-permute-start | bytes 86408 | tf_op jit(solution)/shard_map/ppermute | solution.py:20
  122.4 0.6 copy-start.8
  126.4 90.0 %copy-start.4 = (bf16[180,45,80]{0,2,1:T(8,128)(2,1)S(1)}, bf16[180,45,80]{0,2,1:T(8,128)(2,1)}, u32[]{:S(2)}) copy-start(bf16[180,45,80]{0,2,1:T(8,128)(2,1)} %multiply_convert_fusion) | copy-start | bytes 3888004
  126.4 90.0 %copy-start.9 = (bf16[180,1,80]{0,2,1:T(8,128)(2,1)S(1)}, bf16[180,1,80]{0,2,1:T(8,128)(2,1)}, u32[]{:S(2)}) copy-start(bf16[180,1,80]{0,2,1:T(8,128)(2,1)} %copy-done.8) | copy-start | bytes 86404
  126.4 88.1 %collective-permute-start.7 = (bf16[1,47,80]{2,1,0:T(8,128)(2,1)S(1)}, bf16[1,47,80]{2,1,0:T(8,128)(2,1)S(1)}, u32[]{:S(2)}, u32[]{:S(2)}) collective-permute-start(bf16[1,47,80]{2,1,0:T(8,128)(2,1)S(1)} %copy.19), channel_id=1, source_target_pairs={{0,32},{32,64},{64,96},{1,33},{33,65},{65,97},{2,34},{34,66},{66,9... | collective-permute-start | bytes 22568 | tf_op jit(solution)/shard_map/ppermute | solution.py:17
  130.1 84.9 %collective-permute-start.8 = (bf16[1,47,80]{2,1,0:T(8,128)(2,1)S(1)}, bf16[1,47,80]{2,1,0:T(8,128)(2,1)S(1)}, u32[]{:S(2)}, u32[]{:S(2)}) collective-permute-start(bf16[1,47,80]{2,1,0:T(8,128)(2,1)S(1)} %copy.20), channel_id=1, source_target_pairs={{32,0},{64,32},{96,64},{33,1},{65,33},{97,65},{34,2},{66,34},{98,6... | collective-permute-start | bytes 22568 | tf_op jit(solution)/shard_map/ppermute | solution.py:20
  219.1 4.7 %copy-start.11 = (pred[8,6]{0,1:T(8,128)(4,1)S(1)}, pred[8,6]{0,1:T(8,128)(4,1)}, u32[]{:S(2)}) copy-start(pred[8,6]{0,1:T(8,128)(4,1)} %constant.45) | copy-start | bytes 148
Sparse Core Ops, SparseCore 0:
  132.3 252.8 all-reduce.1
where the time goes:
time: 403 us; the launch traced here: 395 us
  waiting for transfers between devices  187 us (46%)
  blocking collectives  81.6 us (20%)
  local copies, waits for them, and re-layouts  37.2 us (9%)
  matrix products  26.9 us (7%)
  other arithmetic  25.9 us (6%)
  starting transfers between devices  19.2 us (5%)
  between operations  17.1 us (4%)
    psum x1, waiting for transfers between devices, local(): lax.psum((partial_grad, local_total), ('member', 'lat', 'lon'))  152 us
    psum x1, blocking collectives, local(): lax.psum((partial_grad, local_total), ('member', 'lat', 'lon'))  81.6 us
    ppermute x1, waiting for transfers between devices, partner(): return lax.ppermute(value, axis, pairs)  26.6 us
    ppermute x4, starting transfers between devices, padded(): lax.ppermute(lax.slice_in_dim(block, block.shape[dim] - width, None, axis...  16.2 us
    conv_general_dilated x2, matrix products, stencil_filter_step(): lax.conv_general_dilated(haloed_grid_array[None], weights_hwio, (1, 1), '...  14 us
    dot_general x9, matrix products, tap_products(): lax.dot_general(window, flat_grad, (((0,), (0,)), ((), ())), preferred_el...  12.9 us
    conv_general_dilated x5, local copies, waits for them, and re-layouts, stencil_filter_step(): lax.conv_general_dilated(haloed_grid_array[None], weights_hwio, (1, 1), '...  11.6 us
  transfers between devices with their start and end apart: 10, of which 6 were waited for; matrix products, arithmetic and copies ran while one was open for 9% of the time, Pallas kernels for 0%

commit v1 on v0

--- a/solution.py
+++ b/solution.py
@@ -107,7 +107,7 @@
         jnp.bfloat16
     )
     partial_grad = tap_products(haloed_grid_array, cotangent)
-    summed_grad, total = lax.psum((partial_grad, local_total), ("member", "lat", "lon"))
+    summed_grad, total = lax.psum(lax.psum((partial_grad, local_total), ("lat", "lon")), "member")
     objective_mean = total / (total_rows * total_cols)
     filter_weights_slope = summed_grad / math.sqrt(2.0 * total_rows * total_cols)
     return (predicted_outputs[None], objective_mean, hidden_state_slope[None], filter_weights_slope)

time: 403 us -> 1330 us (3.30)
  waiting for transfers between devices: 187 us -> 862 us
  blocking collectives: 81.6 us -> 334 us
    psum x1 -> x2, waiting for transfers between devices: 152 us -> 828 us  [the longest x1 802 us: local(): lax.psum((partial_grad, local_total), ('lat', 'lon'))]
    psum x1 -> x2, blocking collectives: 81.6 us -> 334 us  [the longest x1 329 us: local(): lax.psum((partial_grad, local_total), ('lat', 'lon'))]
  transfers between devices with their start and end apart: 10 -> 11, of which waited for: 6 -> 6; matrix products, arithmetic and copies ran while one was open for 9% -> 3% of each run, Pallas kernels for 0% -> 0%
where the time goes in v1:
time: 1330 us; the launch traced here: 1320 us
  waiting for transfers between devices  862 us (65%)
  blocking collectives  334 us (25%)
  local copies, waits for them, and re-layouts  37.1 us (3%)
  other arithmetic  27.4 us (2%)
  matrix products  27 us (2%)
  starting transfers between devices  19.2 us (1%)
  between operations  17 us (1%)
    psum x1, waiting for transfers between devices, local(): lax.psum((partial_grad, local_total), ('lat', 'lon'))  802 us
    psum x1, blocking collectives, local(): lax.psum((partial_grad, local_total), ('lat', 'lon'))  329 us
  transfers between devices with their start and end apart: 11, of which 6 were waited for; matrix products, arithmetic and copies ran while one was open for 3% of the time, Pallas kernels for 0%

profile of v1, /device:TPU:1, one launch (start us, length us, event | category | flops | bytes accessed | tf_op | source)
XLA Modules:
  0.0 1323.7 jit_solution(8460079494731881473)
XLA Ops:
  7.2 0.0 all-reduce.3.cloned.1.call-start
  7.2 1.0 fusion.76
  8.2 4.4 collective-permute-start
  12.6 1.2 collective-permute-done
  13.7 3.8 collective-permute-done.1
  17.6 1.0 pad_maximum_fusion.5
  18.6 3.1 collective-permute-start.2
  21.7 1.3 collective-permute-start.3
  23.0 3.3 collective-permute-done.3
  26.3 1.0 maximum_bitcast_fusion
  27.3 0.2 pad
  27.5 0.6 copy.17
  28.1 0.2 slice.78
  28.3 6.8 broadcast_select_fusion
  35.1 6.2 copy.18
  41.3 4.4 fusion.3
  45.7 0.4 collective-permute-start.4
  46.1 1.7 copy.27
  47.8 4.5 reshape_squeeze.3
  52.3 0.6 cosine_reduce_fusion
  53.6 0.1 cosine_divide_fusion
  53.7 4.4 maximum_maximum_fusion
  58.0 26.3 %collective-permute-done.4 = bf16[180,45,80]{0,2,1:T(8,128)(2,1)} collective-permute-done((bf16[180,45,80]{0,2,1:T(8,128)(2,1)}, bf16[180,45,80]{0,2,1:T(8,128)(2,1)}, u32[]{:S(2)}, u32[]{:S(2)}) %collective-permute-start.4) | collective-permute-done | bytes 1296032 | tf_op jit(solution)/shard_map/ppermute | solution.py:28
  84.3 3.6 multiply_reduce_fusion
  87.9 0.6 add_sqrt_fusion.1
  88.6 4.8 multiply_convert_fusion
  93.4 4.7 copy.26
  98.1 3.0 fusion.44
  101.1 0.3 copy-done.7
  101.4 0.8 fusion.47
  102.2 0.8 fusion.50
  103.0 0.8 copy-done.6
  103.9 1.3 fusion.53
  105.1 1.3 fusion.56
  106.4 1.3 fusion.59
  107.7 4.2 reshape.50
  111.9 5.5 collective-permute-start.5
  117.4 3.1 convolution_bitcast_fusion
  120.5 0.8 fusion.62
  121.3 0.8 fusion.65
  122.2 0.8 pad_maximum_fusion.2
  123.0 0.0 all-reduce.3.cloned.1.call-update
  123.0 0.0 all-reduce.5.cloned.1.call-start
  123.0 1.9 pad_maximum_fusion.1
  124.9 1.4 fusion.77
  126.3 1.7 copy.19
  128.0 3.1 collective-permute-start.7
  131.2 0.4 copy.20
  131.6 1.3 collective-permute-start.8
  132.9 329.4 %psum.28 = f32[]{:T(128)} all-reduce(f32[]{:T(128)} %get-tuple-element.17), channel_id=1, replica_groups=mesh['member'=2,'lat'=4,'lon'=32] {'lat','lon'}, use_global_device_ids=true, to_apply=%region_4.0 | all-reduce | flops 1 | bytes 8 | tf_op jit(solution)/shard_map/psum | solution.py:110
  462.3 4.4 psum.29
  467.3 0.5 copy.21
  467.8 1.4 copy.22
  469.2 2.4 maximum_bitcast_fusion.1
  471.6 0.4 pad.2
  472.0 3.5 copy.24
  475.5 1.3 slice.84
  476.9 802.0 %all-reduce.3.cloned.1.call-done = f32[3,3,128,80]{2,3,1,0:T(8,128)} async-done(((f32[3,3,128,80]{2,3,1,0:T(8,128)}), f32[3,3,128,80]{2,3,1,0:T(8,128)}) %all-reduce.3.cloned.1.call-update) | async-done | bytes 368656 | tf_op jit(solution)/shard_map/psum | solution.py:110
  1278.8 0.0 all-reduce.5.cloned.1.call-update
  1278.8 7.1 select_convert_fusion
  1286.0 0.6 copy.25
  1286.6 1.5 slice_bitcast_fusion.1
  1288.0 25.7 %all-reduce.5.cloned.1.call-done = f32[3,3,128,80]{2,3,1,0:T(8,128)} async-done(((f32[3,3,128,80]{2,3,1,0:T(8,128)}), f32[3,3,128,80]{2,3,1,0:T(8,128)}) %all-reduce.5.cloned.1.call-update) | async-done | bytes 368656 | tf_op jit(solution)/shard_map/psum | solution.py:110
  1313.8 1.8 broadcast_multiply_fusion
  (26 shorter events, 0.1 us)
Async XLA Ops:
  7.2 21.1 %copy-start = (bf16[3,3,128,80]{2,3,1,0:T(8,128)(2,1)S(1)}, bf16[3,3,128,80]{2,3,1,0:T(8,128)(2,1)}, u32[]{:S(2)}) copy-start(bf16[3,3,128,80]{2,3,1,0:T(8,128)(2,1)} %param.7) | copy-start | bytes 552964
  7.2 19.1 %copy-start.1 = (bf16[1,180,45,128]{3,1,2,0:T(8,128)(2,1)S(1)}, bf16[1,180,45,128]{3,1,2,0:T(8,128)(2,1)}, u32[]{:S(2)}) copy-start(bf16[1,180,45,128]{3,1,2,0:T(8,128)(2,1)} %param.4) | copy-start | bytes 6220804
  7.2 1271.6 %all-reduce.3.cloned.1.call-start = ((), (), s32[]{:S(2)}) async-start(), calls=%async_computation | async-start | bytes 737280 | tf_op jit(solution)/shard_map/psum | solution.py:110
  8.2 5.5 collective-permute-start
  12.6 5.0 collective-permute-start.1
  18.6 4.4 collective-permute-start.2
  21.7 4.6 collective-permute-start.3
  27.5 0.8 copy-start.8
  45.7 38.6 %collective-permute-start.4 = (bf16[180,45,80]{0,2,1:T(8,128)(2,1)}, bf16[180,45,80]{0,2,1:T(8,128)(2,1)}, u32[]{:S(2)}, u32[]{:S(2)}) collective-permute-start(bf16[180,45,80]{0,2,1:T(8,128)(2,1)} %bitcast.6), channel_id=1, source_target_pairs={{0,128},{128,0},{1,129},{129,1},{2,130},{130,2},{3,131},{131,3},{4... | collective-permute-start | bytes 3888008 | tf_op jit(solution)/shard_map/ppermute | solution.py:28
  53.7 30.7 %copy-start.5 = (bf16[180,45,80]{0,2,1:T(8,128)(2,1)S(1)}, bf16[180,45,80]{0,2,1:T(8,128)(2,1)}, u32[]{:S(2)}) copy-start(bf16[180,45,80]{0,2,1:T(8,128)(2,1)} %param.6) | copy-start | bytes 3888004
  98.1 3.0 copy-start.2
  98.1 3.4 copy-start.7
  102.2 1.6 copy-start.6
  111.9 11.1 collective-permute-start.5
  117.4 3.1 copy-start.3
  117.4 5.6 collective-permute-start.6
  123.0 1190.8 %all-reduce.5.cloned.1.call-start = ((), (), s32[]{:S(2)}) async-start(), calls=%async_computation.1 | async-start | bytes 737280 | tf_op jit(solution)/shard_map/psum | solution.py:110
  126.3 342.9 %copy-start.4 = (bf16[180,45,80]{0,2,1:T(8,128)(2,1)S(1)}, bf16[180,45,80]{0,2,1:T(8,128)(2,1)}, u32[]{:S(2)}) copy-start(bf16[180,45,80]{0,2,1:T(8,128)(2,1)} %multiply_convert_fusion) | copy-start | bytes 3888004
  128.0 339.3 %collective-permute-start.7 = (bf16[1,47,80]{2,1,0:T(8,128)(2,1)S(1)}, bf16[1,47,80]{2,1,0:T(8,128)(2,1)S(1)}, u32[]{:S(2)}, u32[]{:S(2)}) collective-permute-start(bf16[1,47,80]{2,1,0:T(8,128)(2,1)S(1)} %copy.19), channel_id=1, source_target_pairs={{0,32},{32,64},{64,96},{1,33},{33,65},{65,97},{2,34},{34,66},{66,9... | collective-permute-start | bytes 22568 | tf_op jit(solution)/shard_map/ppermute | solution.py:17
  131.6 336.2 %collective-permute-start.8 = (bf16[1,47,80]{2,1,0:T(8,128)(2,1)S(1)}, bf16[1,47,80]{2,1,0:T(8,128)(2,1)S(1)}, u32[]{:S(2)}, u32[]{:S(2)}) collective-permute-start(bf16[1,47,80]{2,1,0:T(8,128)(2,1)S(1)} %copy.20), channel_id=1, source_target_pairs={{32,0},{64,32},{96,64},{33,1},{65,33},{97,65},{34,2},{66,34},{98,6... | collective-permute-start | bytes 22568 | tf_op jit(solution)/shard_map/ppermute | solution.py:20
Sparse Core Ops, SparseCore 0:
  123.1 1155.6 all-reduce.2
  1281.6 32.1 all-reduce.4
